TPU v7x, 32 devices: a whole 2x2x4 slice. The times are simulated.
32 devices in a mesh: seq: 8 (over y, x, core), rep: 4 (over z).
Axes of the slice: x: 2, y: 2, z: 4, core: 2. Of those that a mesh axis runs over, the one named last changes fastest.
Arguments:
- histories: bfloat16 [4, 8, 6, 64, 512], P('rep', 'seq'), may hold values from -6 to 6
- cotangents: bfloat16 [4, 8, 6, 64, 512], P('rep', 'seq'), may hold values from -6 to 6
- lengths: int32 [4, 8, 6], P('rep', 'seq'), may hold values from 0 to 64, as said below
- w_in: bfloat16 [512, 2048], replicated, may hold values from -0.25 to 0.25
- w_out: bfloat16 [512, 512], replicated, may hold values from -0.25 to 0.25
Outputs:
- input_grads: bfloat16 [4, 8, 6, 64, 512], P('rep', 'seq')
- w_in_grad: float32 [512, 2048], P('rep', 'seq')
Inputs may be any that keep to these rules, and one draw needn't show every extreme that they name: `lengths`: in each replica group exactly 16 slots have a positive length, every live length is at least 8, and in each group some rank has all 6 of its slots live.
All inputs are finite; a program needn't handle non-finite values.
Results may differ from a plain program's by a relative error of at most 0.025.
Values may be sent and summed in bfloat16 or wider, within the bound.
A program may use at most 64 MiB of HBM per device.

v0:
```python
import jax
import jax.numpy as jnp
from jax import lax
from jax.sharding import PartitionSpec as P

HEADS = 8
CAP = 2


def layer_norm(values):
    average = jnp.mean(values, axis=-1, keepdims=True)
    centered = values - average
    spread = jnp.mean(centered * centered, axis=-1, keepdims=True)
    return centered * lax.rsqrt(spread + 1e-06)


def forward(history, weight_in, weight_out, lengths):
    count_slots, positions, features = history.shape
    head_size = features // HEADS
    normed = layer_norm(history.astype(jnp.float32)).astype(jnp.bfloat16)
    projected = jax.nn.silu(
        jnp.dot(
            normed.reshape(count_slots * positions, features),
            weight_in,
            preferred_element_type=jnp.float32,
        )
    ).astype(jnp.bfloat16)
    projected = projected.reshape(count_slots, positions, 4, HEADS, head_size)
    gate_rows = projected[:, :, 0].reshape(count_slots, positions, features)
    value_rows = projected[:, :, 1]
    query_rows = projected[:, :, 2]
    key_rows = projected[:, :, 3]
    scores = jnp.einsum(
        "cthe,cshe->chts", query_rows, key_rows, preferred_element_type=jnp.float32
    ) * head_size ** (-0.5)
    row_ids = jnp.arange(positions, dtype=jnp.int32)
    allowed = (row_ids[None, :] <= row_ids[:, None])[None, None] & (
        row_ids[None, None, None, :] < lengths[:, None, None, None]
    )
    weights = (
        jnp.where(allowed, jax.nn.silu(scores), 0.0)
        / lengths.astype(jnp.float32)[:, None, None, None]
    ).astype(jnp.bfloat16)
    attended = jnp.einsum(
        "chts,cshe->cthe", weights, value_rows, preferred_element_type=jnp.float32
    ).reshape(count_slots, positions, features)
    gated_out = (layer_norm(attended) * gate_rows.astype(jnp.float32)).astype(jnp.bfloat16)
    mixed_out = jnp.dot(
        gated_out.reshape(count_slots * positions, features),
        weight_out,
        preferred_element_type=jnp.float32,
    )
    return history.astype(jnp.float32) + mixed_out.reshape(count_slots, positions, features)


def cotangent_seed(cotangent, lengths):
    row_ids = jnp.arange(cotangent.shape[1], dtype=jnp.int32)
    valid = row_ids[None, :] < lengths[:, None]
    return jnp.where(valid[:, :, None], cotangent.astype(jnp.float32), 0.0)


def assign(flat_lengths, devices, home_slots):
    slot_total = devices * home_slots
    slot_index = jnp.arange(slot_total, dtype=jnp.int32)
    is_live = flat_lengths > 0
    work_cost = flat_lengths * flat_lengths
    ranking = jnp.where(
        is_live, slot_index - work_cost * slot_total, slot_total * slot_total + slot_index
    )
    ordered = jnp.argsort(ranking)
    leading = ordered[:devices]
    trailing = ordered[devices : 2 * devices][::-1]
    device_ids = jnp.arange(devices, dtype=jnp.int32)
    partner_ids = trailing[(device_ids[None, :] + device_ids[:, None]) % devices]
    clashes = jnp.any(leading[None, :] // home_slots == partner_ids // home_slots, axis=1)
    chosen_shift = jnp.argmin(jnp.where(clashes, devices + device_ids, device_ids))
    usable = jnp.logical_not(jnp.all(clashes))
    partners = trailing[(device_ids + chosen_shift) % devices]
    paired_dest = (
        jnp.zeros(slot_total, jnp.int32).at[leading].set(device_ids).at[partners].set(device_ids)
    )
    paired_slot = jnp.zeros(slot_total, jnp.int32).at[partners].set(1)
    position = jnp.cumsum(is_live.astype(jnp.int32)) - 1
    destination = jnp.where(is_live, jnp.where(usable, paired_dest, position % devices), -1)
    arrival = jnp.where(is_live, jnp.where(usable, paired_slot, position // devices), -1)
    return (destination, arrival)


def shards(histories, cotangents, lengths, w_in, w_out):
    home_slots = histories.shape[2]
    positions = histories.shape[3]
    features = histories.shape[4]
    devices = lax.axis_size("seq")
    device_index = lax.axis_index("seq")
    every_length = lax.all_gather(lengths, "seq", axis=1, tiled=True)
    flat_lengths = every_length.reshape(devices * home_slots)
    destination, arrival = assign(flat_lengths, devices, home_slots)
    my_dest = lax.dynamic_slice_in_dim(destination, device_index * home_slots, home_slots)
    device_ids = jnp.arange(devices, dtype=jnp.int32)
    routing = (my_dest[None, :] == device_ids[:, None]).astype(jnp.bfloat16)
    slot_index = jnp.arange(devices * home_slots, dtype=jnp.int32)
    selected = (destination[None, :] == device_index) & (
        arrival[None, :] == jnp.arange(CAP, dtype=jnp.int32)[:, None]
    )
    arriving = jnp.sum(jnp.where(selected, slot_index[None, :], 0), axis=1)
    arriving_length = flat_lengths[arriving]
    chooser = ((arriving // home_slots)[:, None] == device_ids[None, :]).astype(jnp.bfloat16)

    def outgoing(source):
        spread_out = jnp.dot(
            routing,
            source.reshape(home_slots, positions * features),
            preferred_element_type=jnp.bfloat16,
        )
        return spread_out.reshape(devices, positions, features)

    def collect(source):
        gathered = jnp.dot(
            chooser,
            source.reshape(devices, positions * features),
            preferred_element_type=jnp.bfloat16,
        )
        return gathered.reshape(CAP, positions, features)

    received = lax.all_to_all(outgoing(histories), "seq", split_axis=0, concat_axis=0, tiled=True)
    local_hist = collect(received)
    _, pullback = jax.vjp(
        lambda history_in, weight_in: forward(history_in, weight_in, w_out, arriving_length),
        local_hist,
        w_in,
    )
    local_cot = collect(
        lax.all_to_all(outgoing(cotangents), "seq", split_axis=0, concat_axis=0, tiled=True)
    )
    grad_hist, grad_in = pullback(cotangent_seed(local_cot, arriving_length))
    going_back = jnp.dot(
        chooser.T, grad_hist.reshape(CAP, positions * features), preferred_element_type=jnp.bfloat16
    )
    going_back = going_back.reshape(devices, positions, features)
    returned = lax.all_to_all(going_back, "seq", split_axis=0, concat_axis=0, tiled=True)
    home_grad = jnp.dot(
        routing.T,
        returned.reshape(devices, positions * features),
        preferred_element_type=jnp.bfloat16,
    )
    home_grad = home_grad.reshape(histories.shape)
    gradient = grad_in.astype(jnp.float32)
    column_block = lax.psum_scatter(
        gradient.astype(jnp.bfloat16), "seq", scatter_dimension=1, tiled=True
    )
    w_in_grad = lax.psum_scatter(column_block, "rep", scatter_dimension=0, tiled=True).astype(
        jnp.float32
    )
    return (home_grad, w_in_grad)


def solution(mesh):
    placed = (
        P("rep", "seq", None, None, None),
        P("rep", "seq", None, None, None),
        P("rep", "seq", None),
        P(),
        P(),
    )
    return jax.shard_map(
        shards,
        mesh=mesh,
        in_specs=placed,
        out_specs=(P("rep", "seq", None, None, None), P("rep", "seq")),
        check_vma=False,
    )
```

profile of v0, /device:TPU:0, one launch (start us, length us, event | category | flops | bytes accessed | tf_op | source)
XLA Modules:
  0.0 161.1 jit_solution(15022826188765321410)
XLA Ops:
  7.2 10.5 %all_gather.3 = s32[1,8,6]{2,0,1:T(1,128)S(1)} all-gather(s32[1,1,6]{2,0,1:T(1,128)} %bitcast.158), channel_id=1, replica_groups=mesh['seq'=8,'rep'=4] {'seq'}, dimensions={1}, use_global_device_ids=true | all-gather | bytes 216 | tf_op jit(solution)/shard_map/all_gather | solution.py:95
  19.0 2.0 %sort.17 = (s32[48]{0:T(128)}, s32[48]{0:T(128)S(1)}) sort(s32[48]{0:T(128)S(1)} %add_select_fusion.2, s32[48]{0:T(128)S(1)} %iota.75), dimensions={0}, to_apply=%region_0.1 | sort | flops 288 | bytes 768 | tf_op jit(solution)/shard_map/jit(argsort)/sort | solution.py:70
  28.7 3.5 %all-to-all-start.1 = ((bf16[8,64,512]{2,1,0:T(8,128)(2,1)}), bf16[8,64,512]{2,1,0:T(8,128)(2,1)S(1)}, u32[]{:S(2)}, u32[]{:S(2)}) async-start(bf16[8,64,512]{2,1,0:T(8,128)(2,1)} %copy.169), calls=%async_computation.1 | async-start | bytes 1048576 | tf_op jit(solution)/shard_map/all_to_all | solution.py:125
  33.6 1.5 fusion.32
  36.2 5.6 %all-to-all-done.1 = bf16[8,64,512]{2,1,0:T(8,128)(2,1)S(1)} async-done(((bf16[8,64,512]{2,1,0:T(8,128)(2,1)}), bf16[8,64,512]{2,1,0:T(8,128)(2,1)S(1)}, u32[]{:S(2)}, u32[]{:S(2)}) %all-to-all-start.1) | async-done | bytes 524320 | tf_op jit(solution)/shard_map/all_to_all | solution.py:125
  41.8 4.1 %all-to-all-start = ((bf16[8,64,512]{2,1,0:T(8,128)(2,1)}), bf16[8,64,512]{2,1,0:T(8,128)(2,1)}, u32[]{:S(2)}, u32[]{:S(2)}) async-start(bf16[8,64,512]{2,1,0:T(8,128)(2,1)} %copy.165), calls=%async_computation | async-start | bytes 1048576 | tf_op jit(solution)/shard_map/all_to_all | solution.py:133
  47.5 1.6 %multiply_convert_fusion = (bf16[128,2048]{1,0:T(8,128)(2,1)}, f32[128,2048]{1,0:T(8,128)}) fusion(bf16[128,512]{1,0:T(8,128)(2,1)S(1)} %bitcast.156, bf16[512,2048]{1,0:T(8,128)(2,1)S(1)} %copy-done), kind=kOutput, calls=%fused_computation.30 | convolution fusion | flops 269746176 | bytes 3801088 | tf_op jit(solution)/shard_map/jvp()/dot_general | solution.py:22
  49.1 2.1 %reshape.412 = bf16[2,64,4,8,64]{4,3,2,1,0:T(8,128)(2,1)S(1)} reshape(bf16[128,2048]{1,0:T(8,128)(2,1)} %get-tuple-element.40) | data formatting | bytes 1048576 | tf_op jit(solution)/shard_map/jvp()/reshape | solution.py:28
  51.2 1.1 fusion.66
  52.3 1.2 copy.207
  53.4 1.9 %copy.206 = bf16[2,64,1,8,64]{1,4,3,0,2:T(8,128)(2,1)} copy(bf16[2,64,1,8,64]{4,3,2,1,0:T(8,128)(2,1)} %get-tuple-element.26) | data formatting | bytes 262144
  55.4 2.1 %divide_convert_fusion = (bf16[2,8,64,64]{3,2,1,0:T(8,128)(2,1)S(1)}, f32[2,8,64,64]{3,2,1,0:T(8,128)}) fusion(f32[2]{0:T(128)S(1)} %convert_element_type.139, pred[2,64,64]{2,1,0:T(8,128)(4,1)S(1)} %broadcast_and_fusion, bf16[2,64,1,8,64]{4,3,2,1,0:T(8,128)(2,1)} %get-tuple-element.28, bf16[2,64,1,8,64]{4,3,2,1,0:T(8,128)(2,1)} %get-tuple-element.29), kind=kOutput, calls=%fused_computation.43 | convolution fusion | flops 8912896 | bytes 663560 | tf_op jit(solution)/shard_map/jvp(cthe,cshe->chts)/dot_general | solution.py:33
  58.5 1.5 fusion.7
  60.1 1.4 fusion.6
  63.1 1.2 copy.176
  65.5 1.9 %copy.180 = f32[2,64,1,8,64]{4,3,1,0,2:T(8,128)} copy(bf16[2,64,1,8,64]{1,4,3,0,2:T(8,128)(2,1)} %copy.206) | data formatting | bytes 393216 | tf_op jit(solution)/shard_map/jvp()/convert_element_type | solution.py:47
  67.4 1.1 multiply_reduce_fusion
  68.7 1.9 %reshape.413 = f32[128,512]{1,0:T(8,128)} reshape(f32[2,64,8,64]{3,2,1,0:T(8,128)} %copy.181) | data formatting | bytes 524288 | tf_op jit(solution)/shard_map/jvp()/reshape | solution.py:46
  70.6 1.9 %reshape.419 = f32[128,512]{1,0:T(8,128)} reshape(f32[2,64,1,8,64]{4,3,1,0,2:T(8,128)} %copy.180) | data formatting | bytes 524288 | tf_op jit(solution)/shard_map/jvp()/convert_element_type | solution.py:47
  72.5 1.3 fusion.15
  73.9 1.8 %fusion.14 = bf16[2,8,64,64]{3,2,1,0:T(8,128)(2,1)S(1)} fusion(f32[2,8,64,64]{3,2,1,0:T(8,128)} %get-tuple-element.43, bf16[2,64,1,8,64]{1,4,3,0,2:T(8,128)(2,1)} %copy-done.5, f32[2]{0:T(128)S(1)} %convert_element_type.139, pred[2,64,64]{2,1,0:T(8,128)(4,1)S(1)} %broadcast_and_fusion, f32[2,64,8,64]{1,3,2,0:T(8,128)S(1)} %get-tuple-element.45, ...), kind=kOutput, calls=%fused_computation.38 | convolution fusion | flops 9895936 | bytes 1189896 | tf_op jit(solution)/shard_map/transpose(jvp(chts,cshe->cthe))/dot_general | solution.py:44
  76.7 1.7 %add_convert_fusion = f32[2,64,4,8,64]{1,4,3,0,2:T(8,128)} fusion(bf16[2,64,1,8,64]{1,4,3,0,2:T(8,128)(2,1)S(1)} %fusion.16, bf16[2,64,1,8,64]{1,4,3,0,2:T(8,128)(2,1)S(1)} %fusion.5, bf16[2,64,1,8,64]{1,4,3,0,2:T(8,128)(2,1)S(1)} %fusion.4, bf16[2,64,1,8,64]{1,4,3,0,2:T(8,128)(2,1)S(1)} %fusion.3), kind=kLoop, calls=%fused_computation.29 | loop fusion | flops 1048576 | bytes 1572864 | tf_op jit(solution)/shard_map/transpose(jvp())/convert_element_type | solution.py:27
  78.4 3.8 %copy.188 = f32[2,64,4,8,64]{4,3,2,1,0:T(8,128)} copy(f32[2,64,4,8,64]{1,4,3,0,2:T(8,128)} %add_convert_fusion) | data formatting | bytes 2097152 | tf_op jit(solution)/shard_map/transpose(jvp())/convert_element_type | solution.py:27
  82.2 2.1 %reshape.420 = f32[128,2048]{1,0:T(8,128)S(1)} reshape(f32[2,64,4,8,64]{4,3,2,1,0:T(8,128)} %copy.188) | data formatting | bytes 2097152 | tf_op jit(solution)/shard_map/transpose(jvp())/convert_element_type | solution.py:27
  84.3 3.4 %convolution_convert_fusion = bf16[512,2048]{1,0:T(8,128)(2,1)} fusion(bf16[128,512]{1,0:T(8,128)(2,1)} %bitcast.157, f32[128,2048]{1,0:T(8,128)} %get-tuple-element.41, f32[128,2048]{1,0:T(8,128)S(1)} %reshape.420), kind=kOutput, calls=%fused_computation.6 | convolution fusion | flops 271843328 | bytes 4325376 | tf_op jit(solution)/shard_map/transpose(jvp())/dot_general | solution.py:22
  87.8 2.1 %bitcast_convert_fusion = f32[2,64,512]{2,1,0:T(8,128)S(1)} fusion(bf16[512,2048]{1,0:T(8,128)(2,1)S(1)} %copy-done, f32[128,2048]{1,0:T(8,128)} %get-tuple-element.41, f32[128,2048]{1,0:T(8,128)S(1)} %reshape.420), kind=kOutput, calls=%fused_computation.139 | convolution fusion | flops 270925824 | bytes 4456448 | tf_op jit(solution)/shard_map/transpose(jvp())/dot_general | solution.py:22
  91.1 1.5 fusion.64
  92.7 1.4 fusion.21
  95.0 3.9 %all-to-all-start.2 = ((bf16[8,64,512]{2,1,0:T(8,128)(2,1)}), bf16[8,64,512]{2,1,0:T(8,128)(2,1)S(1)}, u32[]{:S(2)}, u32[]{:S(2)}) async-start(bf16[8,64,512]{2,1,0:T(8,128)(2,1)} %copy.195), calls=%async_computation.2 | async-start | bytes 1048576 | tf_op jit(solution)/shard_map/all_to_all | solution.py:140
  98.9 31.5 %reduce-scatter.3.cloned.1.call-done = bf16[512,256]{1,0:T(8,128)(2,1)} async-done(((bf16[512,2048]{1,0:T(8,128)(2,1)}), bf16[512,256]{1,0:T(8,128)(2,1)}) %reduce-scatter.3.cloned.1.call-update) | async-done | bytes 262160 | tf_op jit(solution)/shard_map/reduce_scatter | solution.py:148
  131.8 21.0 %reduce-scatter.5.cloned.1.call-done = bf16[128,256]{1,0:T(8,128)(2,1)} async-done(((bf16[512,256]{1,0:T(8,128)(2,1)}), bf16[128,256]{1,0:T(8,128)(2,1)}) %reduce-scatter.5.cloned.1.call-update) | async-done | bytes 65552 | tf_op jit(solution)/shard_map/reduce_scatter | solution.py:151
  152.7 1.5 convert_element_type.161
  (109 shorter events, 20.7 us)
Async XLA Ops:
  7.2 40.3 %copy-start = (bf16[512,2048]{1,0:T(8,128)(2,1)S(1)}, bf16[512,2048]{1,0:T(8,128)(2,1)}, u32[]{:S(2)}) copy-start(bf16[512,2048]{1,0:T(8,128)(2,1)} %param.8) | copy-start | bytes 6291460
  21.3 6.0 %copy-start.9 = (bf16[1,1,6,64,512]{4,3,2,1,0:T(8,128)(2,1)S(1)}, bf16[1,1,6,64,512]{4,3,2,1,0:T(8,128)(2,1)}, u32[]{:S(2)}) copy-start(bf16[1,1,6,64,512]{4,3,2,1,0:T(8,128)(2,1)} %param.5) | copy-start | bytes 1179652
  28.7 13.1 %all-to-all-start.1 = ((bf16[8,64,512]{2,1,0:T(8,128)(2,1)}), bf16[8,64,512]{2,1,0:T(8,128)(2,1)S(1)}, u32[]{:S(2)}, u32[]{:S(2)}) async-start(bf16[8,64,512]{2,1,0:T(8,128)(2,1)} %copy.169), calls=%async_computation.1 | async-start | bytes 1048576 | tf_op jit(solution)/shard_map/all_to_all | solution.py:125
  41.8 16.7 %all-to-all-start = ((bf16[8,64,512]{2,1,0:T(8,128)(2,1)}), bf16[8,64,512]{2,1,0:T(8,128)(2,1)}, u32[]{:S(2)}, u32[]{:S(2)}) async-start(bf16[8,64,512]{2,1,0:T(8,128)(2,1)} %copy.165), calls=%async_computation | async-start | bytes 1048576 | tf_op jit(solution)/shard_map/all_to_all | solution.py:133
  46.0 84.5 %reduce-scatter.3.cloned.1.call-start = ((), (), s32[]{:S(2)}) async-start(), calls=%async_computation.5 | async-start | bytes 2359296 | tf_op jit(solution)/shard_map/reduce_scatter | solution.py:148
  47.5 1.7 %copy-start.11 = (bf16[2,64,512]{2,1,0:T(8,128)(2,1)}, bf16[2,64,512]{2,1,0:T(8,128)(2,1)S(1)}, u32[]{:S(2)}) copy-start(bf16[2,64,512]{2,1,0:T(8,128)(2,1)S(1)} %copy.174) | copy-start | bytes 393220
  53.4 4.1 %copy-start.5 = (bf16[2,64,1,8,64]{1,4,3,0,2:T(8,128)(2,1)}, bf16[2,64,1,8,64]{1,4,3,0,2:T(8,128)(2,1)S(1)}, u32[]{:S(2)}) copy-start(bf16[2,64,1,8,64]{1,4,3,0,2:T(8,128)(2,1)S(1)} %copy.207) | copy-start | bytes 393220
  57.5 0.7 copy-start.3
  60.0 1.4 copy-start.10
  61.5 0.7 copy-start.2
  73.9 1.8 %copy-start.8 = (bf16[2,64,1,8,64]{4,3,2,1,0:T(8,128)(2,1)S(1)}, bf16[2,64,1,8,64]{4,3,2,1,0:T(8,128)(2,1)}, u32[]{:S(2)}) copy-start(bf16[2,64,1,8,64]{4,3,2,1,0:T(8,128)(2,1)} %get-tuple-element.29) | copy-start | bytes 393220
  73.9 2.1 %copy-start.7 = (bf16[2,64,1,8,64]{4,3,2,1,0:T(8,128)(2,1)S(1)}, bf16[2,64,1,8,64]{4,3,2,1,0:T(8,128)(2,1)}, u32[]{:S(2)}) copy-start(bf16[2,64,1,8,64]{4,3,2,1,0:T(8,128)(2,1)} %get-tuple-element.28) | copy-start | bytes 393220
  73.9 2.4 %copy-start.1 = (bf16[2,64,1,8,64]{1,4,3,0,2:T(8,128)(2,1)S(1)}, bf16[2,64,1,8,64]{1,4,3,0,2:T(8,128)(2,1)}, u32[]{:S(2)}) copy-start(bf16[2,64,1,8,64]{1,4,3,0,2:T(8,128)(2,1)} %copy.206) | copy-start | bytes 393220
  73.9 2.4 %copy-start.4 = (bf16[2,8,64,64]{3,2,1,0:T(8,128)(2,1)S(1)}, bf16[2,8,64,64]{3,2,1,0:T(8,128)(2,1)}, u32[]{:S(2)}) copy-start(bf16[2,8,64,64]{3,2,1,0:T(8,128)(2,1)} %copy-done.3) | copy-start | bytes 393220
  89.8 0.7 copy-start.6
  95.0 35.5 %all-to-all-start.2 = ((bf16[8,64,512]{2,1,0:T(8,128)(2,1)}), bf16[8,64,512]{2,1,0:T(8,128)(2,1)S(1)}, u32[]{:S(2)}, u32[]{:S(2)}) async-start(bf16[8,64,512]{2,1,0:T(8,128)(2,1)} %copy.195), calls=%async_computation.2 | async-start | bytes 1048576 | tf_op jit(solution)/shard_map/all_to_all | solution.py:140
  98.9 53.9 %reduce-scatter.5.cloned.1.call-start = ((), (), s32[]{:S(2)}) async-start(), calls=%async_computation.6 | async-start | bytes 327680 | tf_op jit(solution)/shard_map/reduce_scatter | solution.py:151
Sparse Core Ops, SparseCore 0:
  87.9 42.5 reduce-scatter.2
  132.7 19.9 reduce-scatter.4
where the time goes:
time: 162 us; the launch traced here: 161 us
  waiting for transfers between devices  58.2 us (36%)
  local copies, waits for them, and re-layouts  32.6 us (20%)
  matrix products  19.3 us (12%)
  between operations  15.2 us (9%)
  other arithmetic  13.6 us (8%)
  starting transfers between devices  11.8 us (7%)
  blocking collectives  10.5 us (6%)
    reduce_scatter x1, waiting for transfers between devices, shards(): lax.psum_scatter(gradient.astype(jnp.bfloat16), 'seq', scatter_dimension=...  31.5 us
    reduce_scatter x1, waiting for transfers between devices, shards(): lax.psum_scatter(column_block, 'rep', scatter_dimension=0, tiled=True)  21 us
    all_gather x1, blocking collectives, shards(): every_length = lax.all_gather(lengths, 'seq', axis=1, tiled=True)  10.5 us
    dot_general x3, matrix products, forward(): jnp.dot(normed.reshape(count_slots * positions, features), weight_in, pre...  7.16 us
    unnamed x27, local copies, waits for them, and re-layouts  6.11 us
    convert_element_type x2, local copies, waits for them, and re-layouts, forward(): projected = jax.nn.silu(jnp.dot(normed.reshape(count_slots * positions, f...  5.86 us
    all_to_all x1, waiting for transfers between devices, shards(): lax.all_to_all(outgoing(histories), 'seq', split_axis=0, concat_axis=0, t...  5.63 us
    all_to_all x1, starting transfers between devices, shards(): lax.all_to_all(outgoing(cotangents), 'seq', split_axis=0, concat_axis=0,...  4.14 us
  transfers between devices with their start and end apart: 5, of which 3 were waited for; matrix products, arithmetic and copies ran while one was open for 14% of the time, Pallas kernels for 0%

commit v1 on v0

v1 whole, which is shorter than its diff:
```python
import functools

import jax
import jax.numpy as jnp
from jax import lax
from jax.experimental import pallas as pl
from jax.experimental.pallas import tpu as pltpu
from jax.sharding import PartitionSpec as P

HEADS = 8
GROUP = 4
CHUNKS = 2
MESH = pl.DeviceIdType.MESH
F32 = jnp.float32
BF16 = jnp.bfloat16


def dot(left, right, left_dim, right_dim):
    return lax.dot_general(
        left, right, (((left_dim,), (right_dim,)), ((), ())), preferred_element_type=F32
    )


def norm_parts(values):
    average = jnp.mean(values, axis=-1, keepdims=True)
    centered = values - average
    spread = jnp.mean(centered * centered, axis=-1, keepdims=True)
    scale = lax.rsqrt(spread + 1e-06)
    return centered * scale, scale


def norm_back(normed, scale, cotangent):
    average = jnp.mean(cotangent, axis=-1, keepdims=True)
    along = jnp.mean(cotangent * normed, axis=-1, keepdims=True)
    return scale * (cotangent - average - normed * along)


def local_body(slots, positions, features, lens_ref, hist_hbm, cot_hbm, win_hbm, wout_hbm,
               emit, finish, hist, cot, win, wout, normed, normed_t, proj, slope, dgate,
               dproj, sems):
    rows = slots * positions
    head = features // HEADS
    width = GROUP * head
    quads = HEADS // GROUP
    block = 256
    copies = [
        pltpu.make_async_copy(hist_hbm, hist, sems.at[0]),
        pltpu.make_async_copy(win_hbm, win, sems.at[1]),
        pltpu.make_async_copy(cot_hbm, cot, sems.at[2]),
        pltpu.make_async_copy(wout_hbm, wout, sems.at[3]),
    ]
    for copy in copies:
        copy.start()
    row_ids = lax.broadcasted_iota(jnp.int32, (positions, 1), 0)
    copies[0].wait()
    scales = []
    for slot in range(slots):
        part, scale = norm_parts(hist[slot].astype(F32))
        scales.append(scale)
        normed[slot * positions:(slot + 1) * positions, :] = part.astype(BF16)
    copies[1].wait()

    @pl.loop(0, 4 * features // block)
    def _(step):
        columns = pl.ds(pl.multiple_of(step * block, block), block)
        out = dot(normed[...], win[:, columns], 1, 0)
        gate = jax.nn.sigmoid(out)
        proj[:, columns] = (out * gate).astype(BF16)
        slope[:, columns] = gate * (1.0 + out * (1.0 - gate))

    copies[2].wait()
    for slot in range(slots):
        valid = row_ids < lens_ref[0, 0, slot]
        cot[slot] = jnp.where(valid, cot[slot], jnp.zeros((), BF16))
    copies[3].wait()
    dgate[...] = dot(cot[...].reshape(rows, features), wout[...], 1, 1).astype(BF16)

    time_ids = lax.broadcasted_iota(jnp.int32, (positions, width), 0)
    key_ids = lax.broadcasted_iota(jnp.int32, (positions, width), 1) % positions
    causal = key_ids <= time_ids
    lane_head = lax.broadcasted_iota(jnp.int32, (positions, width), 1) // head

    def spread_heads(values):
        zero = jnp.zeros((), values.dtype)
        return jnp.concatenate(
            [jnp.where(lane_head == h, values, zero) for h in range(GROUP)], axis=0
        )

    def gather_heads(values):
        total = values[0:positions]
        for h in range(1, GROUP):
            total = jnp.where(lane_head == h, values[h * positions:(h + 1) * positions], total)
        return total

    def columns_of(kind, quad):
        return slice(kind * features + quad * width, kind * features + (quad + 1) * width)

    for slot in range(slots):
        at = slice(slot * positions, (slot + 1) * positions)
        length = lens_ref[0, 0, slot]
        allowed = causal & (key_ids < length)
        per_length = 1.0 / jnp.full((1, width), jnp.maximum(length, 1), jnp.int32).astype(F32)
        weight_of, slope_of, query_of, keys_of, values_of, attended = [], [], [], [], [], []
        for quad in range(quads):
            query = proj[at, columns_of(2, quad)]
            keys = spread_heads(proj[at, columns_of(3, quad)])
            values = spread_heads(proj[at, columns_of(1, quad)])
            scores = dot(query, keys, 1, 1) * head ** (-0.5)
            gate = jax.nn.sigmoid(scores)
            weights = (jnp.where(allowed, scores * gate, 0.0) * per_length).astype(BF16)
            grade = jnp.where(allowed, gate * (1.0 + scores * (1.0 - gate)), 0.0)
            attended.append(dot(weights, values, 1, 0))
            weight_of.append(weights)
            slope_of.append(grade * (per_length * head ** (-0.5)))
            query_of.append(query)
            keys_of.append(keys)
            values_of.append(values)
        normal, scale = norm_parts(jnp.concatenate(attended, axis=1))
        grad = dgate[at, :].astype(F32)
        gates = proj[at, 0:features].astype(F32)
        dproj[at, 0:features] = (
            (grad * normal).astype(BF16).astype(F32) * slope[at, 0:features]
        ).astype(BF16)
        d_att = norm_back(normal, scale, grad * gates).astype(BF16)
        for quad in range(quads):
            d_quad = d_att[:, quad * width:(quad + 1) * width]
            d_values = gather_heads(dot(weight_of[quad], d_quad, 0, 0))
            d_weights = dot(d_quad, values_of[quad], 1, 1).astype(BF16).astype(F32)
            d_scores = (d_weights * slope_of[quad]).astype(BF16)
            d_query = dot(d_scores, keys_of[quad], 1, 0)
            d_keys = gather_heads(dot(d_scores, query_of[quad], 0, 0))
            for kind, value in ((1, d_values), (2, d_query), (3, d_keys)):
                columns = columns_of(kind, quad)
                dproj[at, columns] = (
                    value.astype(BF16).astype(F32) * slope[at, columns]
                ).astype(BF16)

    normed_t[...] = normed[...].T
    emit(normed_t, dproj)
    for half in range(features // block):
        columns = slice(half * block, (half + 1) * block)
        dgate[:, columns] = dot(dproj[...], win[columns, :], 1, 1).astype(BF16)
    for slot in range(slots):
        at = slice(slot * positions, (slot + 1) * positions)
        grad = norm_back(*norm_parts(hist[slot].astype(F32)), dgate[at, :].astype(F32))
        finish(slot, (cot[slot].astype(F32) + grad).astype(BF16))


def local_scratch(slots, positions, features):
    rows = slots * positions
    return [
        pltpu.VMEM((slots, positions, features), BF16),
        pltpu.VMEM((slots, positions, features), BF16),
        pltpu.VMEM((features, 4 * features), BF16),
        pltpu.VMEM((features, features), BF16),
        pltpu.VMEM((rows, features), BF16),
        pltpu.VMEM((features, rows), BF16),
        pltpu.VMEM((rows, 4 * features), BF16),
        pltpu.VMEM((rows, 4 * features), F32),
        pltpu.VMEM((rows, features), BF16),
        pltpu.VMEM((rows, 4 * features), BF16),
        pltpu.SemaphoreType.DMA((4,)),
    ]


def local_kernel(slots, positions, features, blocked, lens_ref, hist_hbm, cot_hbm, win_hbm,
                 wout_hbm, grad_ref, part_ref, *scratch):
    def emit(normed_t, dproj):
        if not blocked:
            block = 256
            for step in range(4 * features // block):
                columns = slice(step * block, (step + 1) * block)
                part_ref[:, columns] = dot(normed_t[...], dproj[:, columns], 1, 0).astype(BF16)
            return
        ranks, groups = blocked
        width = 4 * features // ranks
        piece = features // groups // CHUNKS

        @pl.loop(0, ranks)
        def _(rank):
            columns = pl.ds(pl.multiple_of(rank * width, width), width)
            total = dot(normed_t[...], dproj[:, columns], 1, 0).astype(BF16)
            for group in range(groups):
                for chunk in range(CHUNKS):
                    start = (group * CHUNKS + chunk) * piece
                    part_ref[chunk, rank, group * piece:(group + 1) * piece, :] = total[
                        start:start + piece
                    ]

    def finish(slot, value):
        grad_ref[0, 0, slot] = value

    local_body(slots, positions, features, lens_ref, hist_hbm.at[0, 0], cot_hbm.at[0, 0],
               win_hbm, wout_hbm, emit, finish, *scratch)


def reduce_kernel(groups, part_ref, out_ref, recv0, acc0, recv1, acc1, recv2, acc2, recv3,
                  s0, r0, s1, r1, s2, r2, s3, r3):
    chunks = part_ref.shape[0]
    piece = part_ref.shape[2] // groups
    me, rep = lax.axis_index("seq"), lax.axis_index("rep")
    core = me % 2
    x_at = (me // 2) % 2
    y_at = me // 4
    a_at = x_at + core * (y_at - x_at)
    b_at = y_at + core * (x_at - y_at)
    a_step, b_step = 1 + core, 2 - core
    twin = me + 1 - 2 * core
    a_peer = me + 2 * a_step * (1 - 2 * a_at)
    b_peer = me + 2 * b_step * (1 - 2 * b_at)
    reps = [(rep + d) % groups for d in range(1, groups)]
    barrier = pltpu.get_barrier_semaphore()
    for peer in (twin, a_peer, b_peer):
        pl.semaphore_signal(barrier, inc=1, device_id={"seq": peer}, device_id_type=MESH)
    for peer in reps:
        pl.semaphore_signal(barrier, inc=1, device_id={"rep": peer}, device_id_type=MESH)
    pl.semaphore_wait(barrier, 3 + len(reps))

    def send(source, target, sent, got, peer):
        copy = pltpu.make_async_remote_copy(
            src_ref=source, dst_ref=target, send_sem=sent, recv_sem=got,
            device_id=peer, device_id_type=MESH,
        )
        copy.start()
        return copy

    def add(left, right):
        return (left.astype(F32) + right.astype(F32)).astype(BF16)

    def chip(a, b):
        return a * a_step + b * b_step

    order = ((1 - a_at, 1 - b_at), (1 - a_at, b_at), (a_at, 1 - b_at), (a_at, b_at))
    first, along, across, last = {}, {}, {}, {}
    for k in range(chunks):
        for i, (a, b) in enumerate(order[j] for j in (0, 2, 1, 3)):
            first[k, i] = send(part_ref.at[k, 2 * chip(a, b) + 1 - core], recv0.at[k, i],
                               s0.at[k, i], r0.at[k, i], {"seq": twin})


    def stage_core(k, i):
        a, b = order[i]
        first[k, i].wait_recv()
        acc0[k, i] = add(part_ref[k, 2 * chip(a, b) + core], recv0[k, i])

    for step in range(chunks + 3):
        k = step
        if k < chunks:
            for i in range(2):
                stage_core(k, i)
                along[k, i] = send(acc0.at[k, i], recv1.at[k, i], s1.at[k, i], r1.at[k, i],
                                   {"seq": a_peer})
            for i in range(2, 4):
                stage_core(k, i)
        k = step - 1
        if 0 <= k < chunks:
            along[k, 0].wait_recv()
            acc1[k, 0] = add(acc0[k, 2], recv1[k, 0])
            across[k] = send(acc1.at[k, 0], recv2.at[k], s2.at[k], r2.at[k], {"seq": b_peer})
            along[k, 1].wait_recv()
            acc1[k, 1] = add(acc0[k, 3], recv1[k, 1])
        k = step - 2
        if 0 <= k < chunks:
            across[k].wait_recv()
            acc2[k] = add(acc1[k, 1], recv2[k])
            for d, peer in enumerate(reps):
                rows = pl.ds(pl.multiple_of(peer * piece, piece), piece)
                last[k, d] = send(acc2.at[k, rows], recv3.at[k, d], s3.at[k, d], r3.at[k, d],
                                  {"rep": peer})
        k = step - 3
        if 0 <= k < chunks:
            rows = pl.ds(pl.multiple_of(rep * piece, piece), piece)
            total = acc2[k, rows].astype(F32)
            for d in range(len(reps)):
                last[k, d].wait_recv()
                total = total + recv3[k, d].astype(F32)
            out_ref[k * piece:(k + 1) * piece, :] = total
    for copies in (first, along, across, last):
        for copy in copies.values():
            copy.wait_send()


def shards(histories, cotangents, lengths, w_in, w_out):
    slots, positions, features = histories.shape[2:]
    ranks, groups = lax.axis_size("seq"), lax.axis_size("rep")
    width = 4 * features // ranks
    tall = features // groups
    fast = ranks == 8 and groups == 4 and width % 128 == 0 and tall % (16 * CHUNKS) == 0
    if fast:
        part_shape = (CHUNKS, ranks, features // CHUNKS, width)
    else:
        part_shape = (features, 4 * features)
    anywhere = pl.BlockSpec(memory_space=pl.ANY)
    inside = pl.BlockSpec(memory_space=pltpu.VMEM)
    grads, part = pl.pallas_call(
        functools.partial(local_kernel, slots, positions, features,
                          (ranks, groups) if fast else None),
        out_shape=(jax.ShapeDtypeStruct(histories.shape, BF16),
                   jax.ShapeDtypeStruct(part_shape, BF16)),
        in_specs=[pl.BlockSpec(memory_space=pltpu.SMEM)] + [anywhere] * 4,
        out_specs=(inside, inside),
        scratch_shapes=local_scratch(slots, positions, features),
        name="local",
    )(lengths, histories, cotangents, w_in, w_out)
    if not fast:
        column_block = lax.psum_scatter(part, "seq", scatter_dimension=1, tiled=True)
        total = lax.psum_scatter(column_block, "rep", scatter_dimension=0, tiled=True)
        return grads, total.astype(F32)
    tile = features // CHUNKS
    shapes = [
        (CHUNKS, 4, tile, width), (CHUNKS, 4, tile, width),
        (CHUNKS, 2, tile, width), (CHUNKS, 2, tile, width),
        (CHUNKS, tile, width), (CHUNKS, tile, width),
        (CHUNKS, groups - 1, tile // groups, width),
    ]
    counts = [(CHUNKS, 4), (CHUNKS, 2), (CHUNKS,), (CHUNKS, groups - 1)]
    total = pl.pallas_call(
        functools.partial(reduce_kernel, groups),
        out_shape=jax.ShapeDtypeStruct((tall, width), F32),
        in_specs=[inside],
        out_specs=inside,
        scratch_shapes=[pltpu.VMEM(shape, BF16) for shape in shapes]
        + [pltpu.SemaphoreType.DMA(count) for count in counts for _ in range(2)],
        compiler_params=pltpu.CompilerParams(collective_id=0, has_side_effects=True),
        name="reduce",
    )(part)
    return grads, total


def solution(mesh):
    placed = (
        P("rep", "seq", None, None, None),
        P("rep", "seq", None, None, None),
        P("rep", "seq", None),
        P(),
        P(),
    )
    return jax.shard_map(
        shards,
        mesh=mesh,
        in_specs=placed,
        out_specs=(P("rep", "seq", None, None, None), P("rep", "seq")),
        check_vma=False,
    )
```

time: 162 us -> 44.3 us (0.27)
  waiting for transfers between devices: 58.2 us -> 0 us
  Pallas kernels: 0 us -> 41.9 us
  local copies, waits for them, and re-layouts: 32.6 us -> 1.57 us
  matrix products: 19.3 us -> 0 us
  between operations: 15.2 us -> 0.65 us
  other arithmetic: 13.6 us -> 0 us
  starting transfers between devices: 11.8 us -> 0 us
  blocking collectives: 10.5 us -> 0 us
    reduce_scatter x2 -> x0, waiting for transfers between devices: 52.5 us -> none  [the longest x1 31.5 us: shards(): lax.psum_scatter(gradient.astype(jnp.bfloat16), 'seq', scatter_dimension=...]
    pallas_call x0 -> x2, Pallas kernels: none -> 41.9 us  [the longest x1 25.1 us: shards(): pl.pallas_call(functools.partial(reduce_kernel, groups), out_shape=jax.Sh...]
    dot_general x16 -> x0, matrix products: 19.3 us -> none  [the longest x3 7.16 us: forward(): jnp.dot(normed.reshape(count_slots * positions, features), weight_in, pre...]
    convert_element_type x8 -> x0, local copies, waits for them, and re-layouts: 12 us -> none  [the longest x2 5.86 us: forward(): projected = jax.nn.silu(jnp.dot(normed.reshape(count_slots * positions, f...]
    all_to_all x3 -> x0, starting transfers between devices: 11.5 us -> none  [the longest x1 4.14 us: shards(): lax.all_to_all(outgoing(cotangents), 'seq', split_axis=0, concat_axis=0,...]
    all_gather x1 -> x0, blocking collectives: 10.5 us -> none  [shards(): every_length = lax.all_gather(lengths, 'seq', axis=1, tiled=True)]
    all_to_all x3 -> x0, waiting for transfers between devices: 5.64 us -> none  [the longest x1 5.63 us: shards(): lax.all_to_all(outgoing(histories), 'seq', split_axis=0, concat_axis=0, t...]
    reduce_sum x6 -> x0, other arithmetic: 4.76 us -> none  [the longest x2 2.84 us: layer_norm(): centered = values - average]
  transfers between devices with their start and end apart: 5 -> 0, of which waited for: 3 -> 0; matrix products, arithmetic and copies ran while one was open for 14% -> 0% of each run, Pallas kernels for 0% -> 0%
where the time goes in v1:
time: 44.3 us; the launch traced here: 44.1 us
  Pallas kernels  41.9 us (95%)
  local copies, waits for them, and re-layouts  1.57 us (4%)
  between operations  0.65 us (1%)
    pallas_call x1, Pallas kernels, shards(): pl.pallas_call(functools.partial(reduce_kernel, groups), out_shape=jax.Sh...  25.1 us
    pallas_call x1, Pallas kernels, shards(): pl.pallas_call(functools.partial(local_kernel, slots, positions, features...  16.8 us
    unnamed x1, local copies, waits for them, and re-layouts  1.57 us

profile of v1, /device:TPU:0, one launch (start us, length us, event | category | flops | bytes accessed | tf_op | source)
XLA Modules:
  0.0 44.1 jit_solution(10735461608849090888)
XLA Ops:
  0.6 16.8 %local.1 = (bf16[1,1,6,64,512]{4,3,2,1,0:T(8,128)(2,1)}, bf16[2,8,256,256]{3,2,1,0:T(8,128)(2,1)}) custom-call(s32[1,1,6]{2,1,0:T(1,128)} %lens_ref.1, bf16[1,1,6,64,512]{4,3,2,1,0:T(8,128)(2,1)} %hist_hbm.1, bf16[1,1,6,64,512]{4,3,2,1,0:T(8,128)(2,1)} %cot_hbm.1, bf16[512,2048]{1,0:T(8,128)(2,1)} %win_hbm.1, bf16[512,512]{1,0:T(8,128)(2,1)} %wout_hbm.1), custom_call_target="tpu_custom_call" | custom-call | tf_op jit(solution)/shard_map/local/pallas_call | solution.py:295
  17.5 25.1 %reduce.1 = f32[128,256]{1,0:T(8,128)} custom-call(bf16[2,8,256,256]{3,2,1,0:T(8,128)(2,1)} %get-tuple-element.5.part_ref), custom_call_target="tpu_custom_call" | custom-call | tf_op jit(solution)/shard_map/reduce/pallas_call | solution.py:317
  42.6 1.6 %copy.8 = f32[128,256]{1,0:T(8,128)} copy(f32[128,256]{1,0:T(8,128)} %reduce.1) | data formatting | bytes 262144

commit v2 on v1

v2 whole, which is shorter than its diff:
```python
import functools

import jax
import jax.numpy as jnp
from jax import lax
from jax.experimental import pallas as pl
from jax.experimental.pallas import tpu as pltpu
from jax.sharding import PartitionSpec as P

HEADS = 8
GROUP = 4
MESH = pl.DeviceIdType.MESH
F32 = jnp.float32
BF16 = jnp.bfloat16


def dot(left, right, left_dim, right_dim):
    return lax.dot_general(
        left, right, (((left_dim,), (right_dim,)), ((), ())), preferred_element_type=F32
    )


def norm_parts(values):
    average = jnp.mean(values, axis=-1, keepdims=True)
    centered = values - average
    spread = jnp.mean(centered * centered, axis=-1, keepdims=True)
    scale = lax.rsqrt(spread + 1e-06)
    return centered * scale, scale


def norm_back(normed, scale, cotangent):
    average = jnp.mean(cotangent, axis=-1, keepdims=True)
    along = jnp.mean(cotangent * normed, axis=-1, keepdims=True)
    return scale * (cotangent - average - normed * along)


def local_body(slots, positions, features, lens_ref, hist_hbm, cot_hbm, win_hbm, wout_hbm,
               hist, cot, win, wout, normed, normed_t, proj, slope, dgate,
               dproj, kept_weights, kept_grades, sems):
    rows = slots * positions
    head = features // HEADS
    width = GROUP * head
    quads = HEADS // GROUP
    block = 256
    copies = [
        pltpu.make_async_copy(hist_hbm, hist, sems.at[0]),
        pltpu.make_async_copy(win_hbm, win, sems.at[1]),
        pltpu.make_async_copy(cot_hbm, cot, sems.at[2]),
        pltpu.make_async_copy(wout_hbm, wout, sems.at[3]),
    ]
    for copy in copies:
        copy.start()
    row_ids = lax.broadcasted_iota(jnp.int32, (positions, 1), 0)
    copies[0].wait()
    for slot in range(slots):
        part, _ = norm_parts(hist[slot].astype(F32))
        normed[slot * positions:(slot + 1) * positions, :] = part.astype(BF16)
    copies[1].wait()

    @pl.loop(0, 4 * features // block)
    def _(step):
        columns = pl.ds(pl.multiple_of(step * block, block), block)
        out = dot(normed[...], win[:, columns], 1, 0)
        gate = jax.nn.sigmoid(out)
        proj[:, columns] = (out * gate).astype(BF16)
        slope[:, columns] = gate * (1.0 + out * (1.0 - gate))

    copies[2].wait()
    for slot in range(slots):
        valid = row_ids < lens_ref[0, 0, slot]
        cot[slot] = jnp.where(valid, cot[slot], jnp.zeros((), BF16))
    copies[3].wait()
    dgate[...] = dot(cot[...].reshape(rows, features), wout[...], 1, 1).astype(BF16)

    time_ids = lax.broadcasted_iota(jnp.int32, (positions, width), 0)
    key_ids = lax.broadcasted_iota(jnp.int32, (positions, width), 1) % positions
    causal = key_ids <= time_ids
    lane_head = lax.broadcasted_iota(jnp.int32, (positions, width), 1) // head

    def spread_heads(values):
        zero = jnp.zeros((), values.dtype)
        return jnp.concatenate(
            [jnp.where(lane_head == h, values, zero) for h in range(GROUP)], axis=0
        )

    def gather_heads(values):
        total = values[0:positions]
        for h in range(1, GROUP):
            total = jnp.where(lane_head == h, values[h * positions:(h + 1) * positions], total)
        return total

    def columns_of(kind, quad):
        return pl.ds(pl.multiple_of(kind * features + quad * width, width), width)

    for slot in range(slots):
        at = slice(slot * positions, (slot + 1) * positions)
        length = lens_ref[0, 0, slot]
        allowed = causal & (key_ids < length)
        per_length = 1.0 / jnp.full((1, width), jnp.maximum(length, 1), jnp.int32).astype(F32)
        attended = []
        for quad in range(quads):
            query = proj[at, columns_of(2, quad)]
            keys = spread_heads(proj[at, columns_of(3, quad)])
            values = spread_heads(proj[at, columns_of(1, quad)])
            scores = dot(query, keys, 1, 1) * head ** (-0.5)
            gate = jax.nn.sigmoid(scores)
            weights = (jnp.where(allowed, scores * gate, 0.0) * per_length).astype(BF16)
            grade = jnp.where(allowed, gate * (1.0 + scores * (1.0 - gate)), 0.0)
            attended.append(dot(weights, values, 1, 0))
            kept_weights[at, columns_of(0, quad)] = weights
            kept_grades[at, columns_of(0, quad)] = grade * (per_length * head ** (-0.5))
        normal, scale = norm_parts(jnp.concatenate(attended, axis=1))
        grad = dgate[at, :].astype(F32)
        gates = proj[at, 0:features].astype(F32)
        dproj[at, 0:features] = (
            (grad * normal).astype(BF16).astype(F32) * slope[at, 0:features]
        ).astype(BF16)
        dgate[at, :] = norm_back(normal, scale, grad * gates).astype(BF16)

    def backward(quad):
        for slot in range(slots):
            at = slice(slot * positions, (slot + 1) * positions)
            query = proj[at, columns_of(2, quad)]
            keys = spread_heads(proj[at, columns_of(3, quad)])
            values = spread_heads(proj[at, columns_of(1, quad)])
            d_quad = dgate[at, columns_of(0, quad)]
            d_weights = dot(d_quad, values, 1, 1).astype(BF16).astype(F32)
            d_scores = (d_weights * kept_grades[at, columns_of(0, quad)]).astype(BF16)
            d_values = gather_heads(dot(kept_weights[at, columns_of(0, quad)], d_quad, 0, 0))
            d_query = dot(d_scores, keys, 1, 0)
            d_keys = gather_heads(dot(d_scores, query, 0, 0))
            for kind, value in ((1, d_values), (2, d_query), (3, d_keys)):
                columns = columns_of(kind, quad)
                dproj[at, columns] = (
                    value.astype(BF16).astype(F32) * slope[at, columns]
                ).astype(BF16)

    normed_t[...] = normed[...].T

    def grad_block(at):
        columns = slice(at * block, (at + 1) * block)
        dgate[:, columns] = dot(dproj[...], win[columns, :], 1, 1).astype(BF16)

    def finish(slot):
        at = slice(slot * positions, (slot + 1) * positions)
        grad = norm_back(*norm_parts(hist[slot].astype(F32)), dgate[at, :].astype(F32))
        return (cot[slot].astype(F32) + grad).astype(BF16)

    def product(columns):
        return dot(normed_t[...], dproj[:, columns], 1, 0).astype(BF16)

    return backward, product, [functools.partial(grad_block, i) for i in range(features // block)], finish


def local_scratch(slots, positions, features):
    rows = slots * positions
    return [
        pltpu.VMEM((slots, positions, features), BF16),
        pltpu.VMEM((slots, positions, features), BF16),
        pltpu.VMEM((features, 4 * features), BF16),
        pltpu.VMEM((features, features), BF16),
        pltpu.VMEM((rows, features), BF16),
        pltpu.VMEM((features, rows), BF16),
        pltpu.VMEM((rows, 4 * features), BF16),
        pltpu.VMEM((rows, 4 * features), F32),
        pltpu.VMEM((rows, features), BF16),
        pltpu.VMEM((rows, 4 * features), BF16),
        pltpu.VMEM((rows, features), BF16),
        pltpu.VMEM((rows, features), F32),
        pltpu.SemaphoreType.DMA((4,)),
    ]


def local_kernel(slots, positions, features, lens_ref, hist_hbm, cot_hbm, win_hbm, wout_hbm,
                 grad_ref, part_ref, *scratch):
    backward, product, grad_blocks, finish = local_body(
        slots, positions, features, lens_ref, hist_hbm.at[0, 0], cot_hbm.at[0, 0], win_hbm,
        wout_hbm, *scratch)
    for quad in range(HEADS // GROUP):
        backward(quad)
    block = 256
    for step in range(4 * features // block):
        columns = slice(step * block, (step + 1) * block)
        part_ref[:, columns] = product(columns)
    for grad_block in grad_blocks:
        grad_block()
    for slot in range(slots):
        grad_ref[0, 0, slot] = finish(slot)


def fused_kernel(slots, positions, features, groups, lens_ref, hist_hbm, cot_hbm, win_hbm,
                 wout_hbm, grad_ref, out_ref, *refs):
    split = len(local_scratch(slots, positions, features))
    scratch = refs[:split]
    (part, recv0, acc0, recv1, acc1, recv2, acc2, recv3,
     s0, r0, s1, r1, s2, r2, s3, r3) = refs[split:]
    features, width = part.shape[1:]
    tall = features // groups
    me, rep = lax.axis_index("seq"), lax.axis_index("rep")
    core = me % 2
    x_at = (me // 2) % 2
    y_at = me // 4
    a_at = x_at + core * (y_at - x_at)
    b_at = y_at + core * (x_at - y_at)
    a_step, b_step = 1 + core, 2 - core
    twin = me + 1 - 2 * core
    a_peer = me + 2 * a_step * (1 - 2 * a_at)
    b_peer = me + 2 * b_step * (1 - 2 * b_at)
    mirror, swap = 3 - rep, rep + 2 - 4 * (rep // 2)
    beside = rep + 1 - 2 * (rep % 2)
    reps = [mirror, swap, beside]
    barrier = pltpu.get_barrier_semaphore()
    for peer in (twin, a_peer, b_peer):
        pl.semaphore_signal(barrier, inc=1, device_id={"seq": peer}, device_id_type=MESH)
    for peer in reps:
        pl.semaphore_signal(barrier, inc=1, device_id={"rep": peer}, device_id_type=MESH)

    backward, product, grad_blocks, finish = local_body(
        slots, positions, features, lens_ref, hist_hbm.at[0, 0], cot_hbm.at[0, 0], win_hbm,
        wout_hbm, *scratch)
    pl.semaphore_wait(barrier, 3 + len(reps))

    def send(source, target, sent, got, peer):
        copy = pltpu.make_async_remote_copy(
            src_ref=source, dst_ref=target, send_sem=sent, recv_sem=got,
            device_id=peer, device_id_type=MESH,
        )
        copy.start()
        return copy

    def add(left, right):
        return (left.astype(F32) + right.astype(F32)).astype(BF16)

    def chip(a, b):
        return a * a_step + b * b_step

    order = ((1 - a_at, 1 - b_at), (1 - a_at, b_at), (a_at, 1 - b_at), (a_at, b_at))
    first, along, across, last = {}, {}, {}, {}

    def block_of(position, half):
        a, b = order[position]
        rank = 2 * chip(a, b) + half
        return product(pl.ds(pl.multiple_of(rank * width, width), width))

    strips = [pl.ds(pl.multiple_of(z * tall, tall), tall) for z in reps + [rep]]

    backward(1 - core)
    for i, j in enumerate((0, 2, 1, 3)):
        part[i] = block_of(j, 1 - core)
        first[i] = send(part.at[i], recv0.at[i], s0.at[i], r0.at[i], {"seq": twin})
    backward(core)
    for i in range(4):
        own = block_of(i, core)
        first[i].wait_recv()
        acc0[i] = add(own, recv0[i])
        if i < 2:
            for k, strip in enumerate(strips):
                along[i, k] = send(acc0.at[i, strip], recv1.at[i, k], s1.at[i, k],
                                   r1.at[i, k], {"seq": a_peer})

    def stage1(k):
        along[0, k].wait_recv()
        acc1[k] = add(acc0[2, strips[k]], recv1[0, k])
        across[k] = send(acc1.at[k], recv2.at[k], s2.at[k], r2.at[k], {"seq": b_peer})

    def stage2(k):
        along[1, k].wait_recv()
        across[k].wait_recv()
        total = acc0[3, strips[k]].astype(F32) + recv1[1, k].astype(F32) + recv2[k].astype(F32)
        if k < len(reps):
            acc2[k] = total.astype(BF16)
            last[k] = send(acc2.at[k], recv3.at[k], s3.at[k], r3.at[k], {"rep": reps[k]})
            return
        for d in range(len(reps)):
            last[d].wait_recv()
            total = total + recv3[d].astype(F32)
        out_ref[...] = total

    def store(slot):
        grad_ref[0, 0, slot] = finish(slot)

    fill = list(grad_blocks) + [functools.partial(store, slot) for slot in range(slots)]
    fill.pop(0)()
    for stage in (stage1, stage2):
        for k in range(len(strips)):
            stage(k)
            if fill:
                fill.pop(0)()
    for work in fill:
        work()
    for copies in (first, along, across, last):
        for copy in copies.values():
            copy.wait_send()


def leave_kernel(grad_in, total_in, grad_hbm, total_hbm, sems):
    copies = [pltpu.make_async_copy(total_in, total_hbm, sems.at[0]),
              pltpu.make_async_copy(grad_in, grad_hbm, sems.at[1])]
    for copy in copies:
        copy.start()
    for copy in copies:
        copy.wait()


def shards(histories, cotangents, lengths, w_in, w_out):
    slots, positions, features = histories.shape[2:]
    ranks, groups = lax.axis_size("seq"), lax.axis_size("rep")
    width = 4 * features // ranks
    tall = features // groups
    fast = ranks == 8 and groups == 4 and width % 128 == 0 and tall % 16 == 0 and width == GROUP * features // HEADS
    anywhere = pl.BlockSpec(memory_space=pl.ANY)
    inside = pl.BlockSpec(memory_space=pltpu.VMEM)
    in_specs = [pl.BlockSpec(memory_space=pltpu.SMEM)] + [pl.BlockSpec(memory_space=pltpu.HBM)] * 4
    grad_shape = jax.ShapeDtypeStruct(histories.shape, BF16)
    scratch = local_scratch(slots, positions, features)
    operands = (lengths, histories, cotangents, w_in, w_out)
    if not fast:
        grads, part = pl.pallas_call(
            functools.partial(local_kernel, slots, positions, features),
            out_shape=(grad_shape, jax.ShapeDtypeStruct((features, 4 * features), BF16)),
            in_specs=in_specs,
            out_specs=(inside, inside),
            scratch_shapes=scratch,
            name="local",
        )(*operands)
        column_block = lax.psum_scatter(part, "seq", scatter_dimension=1, tiled=True)
        total = lax.psum_scatter(column_block, "rep", scatter_dimension=0, tiled=True)
        return grads, total.astype(F32)
    shapes = [
        (4, features, width), (4, features, width), (4, features, width),
        (2, groups, tall, width), (groups, tall, width), (groups, tall, width),
        (groups - 1, tall, width), (groups - 1, tall, width),
    ]
    counts = [(4,), (2, groups), (groups,), (groups - 1,)]
    total_shape = jax.ShapeDtypeStruct((tall, width), F32)
    grads, total = pl.pallas_call(
        functools.partial(fused_kernel, slots, positions, features, groups),
        out_shape=(grad_shape, total_shape),
        in_specs=in_specs,
        out_specs=(inside, inside),
        scratch_shapes=scratch + [pltpu.VMEM(shape, BF16) for shape in shapes]
        + [pltpu.SemaphoreType.DMA(count) for count in counts for _ in range(2)],
        compiler_params=pltpu.CompilerParams(collective_id=0, has_side_effects=True,
                                             vmem_limit_bytes=32 * 1024 * 1024),
        name="fused",
    )(*operands)
    return pl.pallas_call(
        leave_kernel,
        out_shape=(grad_shape, total_shape),
        in_specs=[inside, inside],
        out_specs=(anywhere, anywhere),
        scratch_shapes=[pltpu.SemaphoreType.DMA((2,))],
        compiler_params=pltpu.CompilerParams(vmem_limit_bytes=4 * 1024 * 1024),
        name="leave",
    )(grads, total)


def solution(mesh):
    placed = (
        P("rep", "seq", None, None, None),
        P("rep", "seq", None, None, None),
        P("rep", "seq", None),
        P(),
        P(),
    )
    return jax.shard_map(
        shards,
        mesh=mesh,
        in_specs=placed,
        out_specs=(P("rep", "seq", None, None, None), P("rep", "seq")),
        check_vma=False,
    )
```

time: 44.3 us -> 36.3 us (0.82)
  Pallas kernels: 41.9 us -> 30 us
  local copies, waits for them, and re-layouts: 1.57 us -> 5.27 us
    pallas_call x2, Pallas kernels: 41.9 us -> 30 us  [the longest x1 29.2 us: shards(): pl.pallas_call(functools.partial(fused_kernel, slots, positions, features...]
    unnamed x1 -> x10, local copies, waits for them, and re-layouts: 1.57 us -> 5.27 us
where the time goes in v2:
time: 36.3 us; the launch traced here: 36 us
  Pallas kernels  30 us (83%)
  local copies, waits for them, and re-layouts  5.27 us (15%)
  between operations  0.65 us (2%)
    pallas_call x1, Pallas kernels, shards(): pl.pallas_call(functools.partial(fused_kernel, slots, positions, features...  29.2 us
    unnamed x10, local copies, waits for them, and re-layouts  5.27 us
    pallas_call x1, Pallas kernels, shards(): pl.pallas_call(leave_kernel, out_shape=(grad_shape, total_shape), in_spec...  0.81 us

profile of v2, /device:TPU:0, one launch (start us, length us, event | category | flops | bytes accessed | tf_op | source)
XLA Modules:
  0.0 36.0 jit_solution(11645047084566762881)
XLA Ops:
  0.6 0.0 copy-start
  0.6 1.6 %copy-done = bf16[512,2048]{1,0:T(8,128)(2,1)S(1)} copy-done((bf16[512,2048]{1,0:T(8,128)(2,1)S(1)}, bf16[512,2048]{1,0:T(8,128)(2,1)}, u32[]{:S(2)}) %copy-start) | copy-done | bytes 2097176
  2.2 0.0 copy-start.1
  2.2 1.0 %copy-done.1 = bf16[512,512]{1,0:T(8,128)(2,1)S(1)} copy-done((bf16[512,512]{1,0:T(8,128)(2,1)S(1)}, bf16[512,512]{1,0:T(8,128)(2,1)}, u32[]{:S(2)}) %copy-start.1) | copy-done | bytes 524312
  3.3 0.0 copy-start.2
  3.3 1.0 %copy-done.2 = bf16[1,1,6,64,512]{4,3,2,1,0:T(8,128)(2,1)S(1)} copy-done((bf16[1,1,6,64,512]{4,3,2,1,0:T(8,128)(2,1)S(1)}, bf16[1,1,6,64,512]{4,3,2,1,0:T(8,128)(2,1)}, u32[]{:S(2)}) %copy-start.2) | copy-done | bytes 393240
  4.3 0.0 copy-start.3
  4.3 1.0 %copy-done.3 = bf16[1,1,6,64,512]{4,3,2,1,0:T(8,128)(2,1)S(1)} copy-done((bf16[1,1,6,64,512]{4,3,2,1,0:T(8,128)(2,1)S(1)}, bf16[1,1,6,64,512]{4,3,2,1,0:T(8,128)(2,1)}, u32[]{:S(2)}) %copy-start.3) | copy-done | bytes 393240
  5.3 0.0 copy-start.4
  5.3 0.7 %copy-done.4 = s32[1,1,6]{2,1,0:T(1,128)S(1)} copy-done((s32[1,1,6]{2,1,0:T(1,128)S(1)}, s32[1,1,6]{2,1,0:T(1,128)}, u32[]{:S(2)}) %copy-start.4) | copy-done | bytes 48
  5.9 29.2 %fused.1 = (bf16[1,1,6,64,512]{4,3,2,1,0:T(8,128)(2,1)S(1)}, f32[128,256]{1,0:T(8,128)S(1)}) custom-call(s32[1,1,6]{2,1,0:T(1,128)S(1)} %copy-done.4, bf16[1,1,6,64,512]{4,3,2,1,0:T(8,128)(2,1)S(1)} %copy-done.2, bf16[1,1,6,64,512]{4,3,2,1,0:T(8,128)(2,1)S(1)} %copy-done.3, bf16[512,2048]{1,0:T(8,128)(2,1)S(1)} %copy-done, bf16[512,512]{1,0:T(8,128)(2,1)S(1)} %copy-done.1), custom_call_target="tpu_custom_call" | custom-call | tf_op jit(solution)/shard_map/fused/pallas_call | solution.py:336
  35.2 0.8 %leave.1 = (bf16[1,1,6,64,512]{4,3,2,1,0:T(8,128)(2,1)}, f32[128,256]{1,0:T(8,128)}) custom-call(bf16[1,1,6,64,512]{4,3,2,1,0:T(8,128)(2,1)S(1)} %get-tuple-element.4.grad_in, f32[128,256]{1,0:T(8,128)S(1)} %get-tuple-element.5.total_in), custom_call_target="tpu_custom_call" | custom-call | tf_op jit(solution)/shard_map/leave/pallas_call | solution.py:347
Async XLA Ops:
  0.6 1.6 %copy-start = (bf16[512,2048]{1,0:T(8,128)(2,1)S(1)}, bf16[512,2048]{1,0:T(8,128)(2,1)}, u32[]{:S(2)}) copy-start(bf16[512,2048]{1,0:T(8,128)(2,1)} %win_hbm.1) | copy-start | bytes 6291460
  2.2 1.0 %copy-start.1 = (bf16[512,512]{1,0:T(8,128)(2,1)S(1)}, bf16[512,512]{1,0:T(8,128)(2,1)}, u32[]{:S(2)}) copy-start(bf16[512,512]{1,0:T(8,128)(2,1)} %wout_hbm.1) | copy-start | bytes 1572868
  3.3 1.0 %copy-start.2 = (bf16[1,1,6,64,512]{4,3,2,1,0:T(8,128)(2,1)S(1)}, bf16[1,1,6,64,512]{4,3,2,1,0:T(8,128)(2,1)}, u32[]{:S(2)}) copy-start(bf16[1,1,6,64,512]{4,3,2,1,0:T(8,128)(2,1)} %hist_hbm.1) | copy-start | bytes 1179652
  4.3 1.0 %copy-start.3 = (bf16[1,1,6,64,512]{4,3,2,1,0:T(8,128)(2,1)S(1)}, bf16[1,1,6,64,512]{4,3,2,1,0:T(8,128)(2,1)}, u32[]{:S(2)}) copy-start(bf16[1,1,6,64,512]{4,3,2,1,0:T(8,128)(2,1)} %cot_hbm.1) | copy-start | bytes 1179652
  5.3 0.7 %copy-start.4 = (s32[1,1,6]{2,1,0:T(1,128)S(1)}, s32[1,1,6]{2,1,0:T(1,128)}, u32[]{:S(2)}) copy-start(s32[1,1,6]{2,1,0:T(1,128)} %lens_ref.1) | copy-start | bytes 76

commit v3 on v2

--- a/solution.py
+++ b/solution.py
@@ -44,32 +44,40 @@
     block = 256
     copies = [
         pltpu.make_async_copy(hist_hbm, hist, sems.at[0]),
-        pltpu.make_async_copy(win_hbm, win, sems.at[1]),
         pltpu.make_async_copy(cot_hbm, cot, sems.at[2]),
-        pltpu.make_async_copy(wout_hbm, wout, sems.at[3]),
+        pltpu.make_async_copy(wout_hbm, wout, sems.at[1]),
     ]
-    for copy in copies:
+
+    def load(step):
+        columns = pl.ds(pl.multiple_of(step * block, block), block)
+        return pltpu.make_async_copy(win_hbm.at[:, columns], win.at[:, columns],
+                                     sems.at[3 + step])
+
+    copies[0].start()
+    for step in range(4 * features // block):
+        load(step).start()
+    for copy in copies[1:]:
         copy.start()
     row_ids = lax.broadcasted_iota(jnp.int32, (positions, 1), 0)
     copies[0].wait()
     for slot in range(slots):
         part, _ = norm_parts(hist[slot].astype(F32))
         normed[slot * positions:(slot + 1) * positions, :] = part.astype(BF16)
-    copies[1].wait()
 
     @pl.loop(0, 4 * features // block)
     def _(step):
         columns = pl.ds(pl.multiple_of(step * block, block), block)
+        load(step).wait()
         out = dot(normed[...], win[:, columns], 1, 0)
         gate = jax.nn.sigmoid(out)
         proj[:, columns] = (out * gate).astype(BF16)
         slope[:, columns] = gate * (1.0 + out * (1.0 - gate))
 
-    copies[2].wait()
+    copies[1].wait()
     for slot in range(slots):
         valid = row_ids < lens_ref[0, 0, slot]
         cot[slot] = jnp.where(valid, cot[slot], jnp.zeros((), BF16))
-    copies[3].wait()
+    copies[2].wait()
     dgate[...] = dot(cot[...].reshape(rows, features), wout[...], 1, 1).astype(BF16)
 
     time_ids = lax.broadcasted_iota(jnp.int32, (positions, width), 0)
@@ -167,7 +175,7 @@
         pltpu.VMEM((rows, 4 * features), BF16),
         pltpu.VMEM((rows, features), BF16),
         pltpu.VMEM((rows, features), F32),
-        pltpu.SemaphoreType.DMA((4,)),
+        pltpu.SemaphoreType.DMA((3 + 4 * features // 256,)),
     ]
 
 
@@ -249,14 +257,14 @@
         part[i] = block_of(j, 1 - core)
         first[i] = send(part.at[i], recv0.at[i], s0.at[i], r0.at[i], {"seq": twin})
     backward(core)
+    early = {0: ((0, 0), (0, 1)), 1: ((1, 0), (0, 2), (1, 1), (0, 3), (1, 2), (1, 3))}
     for i in range(4):
         own = block_of(i, core)
         first[i].wait_recv()
         acc0[i] = add(own, recv0[i])
-        if i < 2:
-            for k, strip in enumerate(strips):
-                along[i, k] = send(acc0.at[i, strip], recv1.at[i, k], s1.at[i, k],
-                                   r1.at[i, k], {"seq": a_peer})
+        for j, k in early.get(i, ()):
+            along[j, k] = send(acc0.at[j, strips[k]], recv1.at[j, k], s1.at[j, k],
+                               r1.at[j, k], {"seq": a_peer})
 
     def stage1(k):
         along[0, k].wait_recv()
@@ -280,12 +288,15 @@
         grad_ref[0, 0, slot] = finish(slot)
 
     fill = list(grad_blocks) + [functools.partial(store, slot) for slot in range(slots)]
-    fill.pop(0)()
-    for stage in (stage1, stage2):
-        for k in range(len(strips)):
-            stage(k)
-            if fill:
-                fill.pop(0)()
+    stages = [None, (stage1, 0), (stage1, 1), (stage2, 0), (stage1, 2), (stage2, 1),
+              (stage1, 3), (stage2, 2), None, (stage2, 3)]
+    counts = [1, 1, 0, 1, 1, 1, 1, 1, slots, 0]
+    for stage, count in zip(stages, counts):
+        if stage:
+            stage[0](stage[1])
+        for work in fill[:count]:
+            work()
+        fill = fill[count:]
     for work in fill:
         work()
     for copies in (first, along, across, last):
@@ -341,7 +352,7 @@
         scratch_shapes=scratch + [pltpu.VMEM(shape, BF16) for shape in shapes]
         + [pltpu.SemaphoreType.DMA(count) for count in counts for _ in range(2)],
         compiler_params=pltpu.CompilerParams(collective_id=0, has_side_effects=True,
-                                             vmem_limit_bytes=32 * 1024 * 1024),
+                                             vmem_limit_bytes=55850000),
         name="fused",
     )(*operands)
     return pl.pallas_call(

time: 36.3 us -> 32 us (0.88)
  local copies, waits for them, and re-layouts: 5.27 us -> 0.65 us
  Pallas kernels: 30 us -> 30.5 us
    unnamed x10 -> x2, local copies, waits for them, and re-layouts: 5.27 us -> 0.65 us
    pallas_call x1, Pallas kernels: 29.2 us -> 29.7 us  [shards(): pl.pallas_call(functools.partial(fused_kernel, slots, positions, features...]
where the time goes in v3:
time: 32 us; the launch traced here: 31.8 us
  Pallas kernels  30.5 us (95%)
  local copies, waits for them, and re-layouts  0.65 us (2%)
  between operations  0.65 us (2%)
    pallas_call x1, Pallas kernels, shards(): pl.pallas_call(functools.partial(fused_kernel, slots, positions, features...  29.7 us
    pallas_call x1, Pallas kernels, shards(): pl.pallas_call(leave_kernel, out_shape=(grad_shape, total_shape), in_spec...  0.81 us
    unnamed x2, local copies, waits for them, and re-layouts  0.65 us

profile of v3, /device:TPU:0, one launch (start us, length us, event | category | flops | bytes accessed | tf_op | source)
XLA Modules:
  0.0 31.8 jit_solution(1183585925448571602)
XLA Ops:
  0.6 0.0 copy-start
  0.6 0.6 %copy-done = s32[1,1,6]{2,1,0:T(1,128)S(1)} copy-done((s32[1,1,6]{2,1,0:T(1,128)S(1)}, s32[1,1,6]{2,1,0:T(1,128)}, u32[]{:S(2)}) %copy-start) | copy-done | bytes 48
  1.3 29.7 %fused.1 = (bf16[1,1,6,64,512]{4,3,2,1,0:T(8,128)(2,1)S(1)}, f32[128,256]{1,0:T(8,128)S(1)}) custom-call(s32[1,1,6]{2,1,0:T(1,128)S(1)} %copy-done, bf16[1,1,6,64,512]{4,3,2,1,0:T(8,128)(2,1)} %hist_hbm.1, bf16[1,1,6,64,512]{4,3,2,1,0:T(8,128)(2,1)} %cot_hbm.1, bf16[512,2048]{1,0:T(8,128)(2,1)} %win_hbm.1, bf16[512,512]{1,0:T(8,128)(2,1)} %wout_hbm.1), custom_call_target="tpu_custom_call" | custom-call | tf_op jit(solution)/shard_map/fused/pallas_call | solution.py:347
  31.0 0.8 %leave.1 = (bf16[1,1,6,64,512]{4,3,2,1,0:T(8,128)(2,1)}, f32[128,256]{1,0:T(8,128)}) custom-call(bf16[1,1,6,64,512]{4,3,2,1,0:T(8,128)(2,1)S(1)} %get-tuple-element.4.grad_in, f32[128,256]{1,0:T(8,128)S(1)} %get-tuple-element.5.total_in), custom_call_target="tpu_custom_call" | custom-call | tf_op jit(solution)/shard_map/leave/pallas_call | solution.py:358
Async XLA Ops:
  0.6 0.7 %copy-start = (s32[1,1,6]{2,1,0:T(1,128)S(1)}, s32[1,1,6]{2,1,0:T(1,128)}, u32[]{:S(2)}) copy-start(s32[1,1,6]{2,1,0:T(1,128)} %lens_ref.1) | copy-start | bytes 76

commit v4 on v3

--- a/solution.py
+++ b/solution.py
@@ -216,17 +216,17 @@
     b_peer = me + 2 * b_step * (1 - 2 * b_at)
     mirror, swap = 3 - rep, rep + 2 - 4 * (rep // 2)
     beside = rep + 1 - 2 * (rep % 2)
-    reps = [mirror, swap, beside]
+    owners, reps = [mirror, beside, swap], [beside, beside, swap]
     barrier = pltpu.get_barrier_semaphore()
     for peer in (twin, a_peer, b_peer):
         pl.semaphore_signal(barrier, inc=1, device_id={"seq": peer}, device_id_type=MESH)
-    for peer in reps:
+    for peer in (beside, swap):
         pl.semaphore_signal(barrier, inc=1, device_id={"rep": peer}, device_id_type=MESH)
 
     backward, product, grad_blocks, finish = local_body(
         slots, positions, features, lens_ref, hist_hbm.at[0, 0], cot_hbm.at[0, 0], win_hbm,
         wout_hbm, *scratch)
-    pl.semaphore_wait(barrier, 3 + len(reps))
+    pl.semaphore_wait(barrier, 5)
 
     def send(source, target, sent, got, peer):
         copy = pltpu.make_async_remote_copy(
@@ -250,14 +250,14 @@
         rank = 2 * chip(a, b) + half
         return product(pl.ds(pl.multiple_of(rank * width, width), width))
 
-    strips = [pl.ds(pl.multiple_of(z * tall, tall), tall) for z in reps + [rep]]
+    strips = [pl.ds(pl.multiple_of(z * tall, tall), tall) for z in owners + [rep]]
 
     backward(1 - core)
     for i, j in enumerate((0, 2, 1, 3)):
         part[i] = block_of(j, 1 - core)
         first[i] = send(part.at[i], recv0.at[i], s0.at[i], r0.at[i], {"seq": twin})
     backward(core)
-    early = {0: ((0, 0), (0, 1)), 1: ((1, 0), (0, 2), (1, 1), (0, 3), (1, 2), (1, 3))}
+    early = {0: ((0, 0),), 1: ((1, 0), (0, 1), (1, 1), (0, 2), (1, 2), (0, 3), (1, 3))}
     for i in range(4):
         own = block_of(i, core)
         first[i].wait_recv()
@@ -275,11 +275,14 @@
         along[1, k].wait_recv()
         across[k].wait_recv()
         total = acc0[3, strips[k]].astype(F32) + recv1[1, k].astype(F32) + recv2[k].astype(F32)
+        if k == 2:
+            last[0].wait_recv()
+            total = total + recv3[0].astype(F32)
         if k < len(reps):
             acc2[k] = total.astype(BF16)
             last[k] = send(acc2.at[k], recv3.at[k], s3.at[k], r3.at[k], {"rep": reps[k]})
             return
-        for d in range(len(reps)):
+        for d in (1, 2):
             last[d].wait_recv()
             total = total + recv3[d].astype(F32)
         out_ref[...] = total

time: 32 us -> 32.7 us (1.022)
  Pallas kernels: 30.5 us -> 31.2 us
    pallas_call x1, Pallas kernels: 29.7 us -> 30.4 us  [shards(): pl.pallas_call(functools.partial(fused_kernel, slots, positions, features...]
where the time goes in v4:
time: 32.7 us; the launch traced here: 32.5 us
  Pallas kernels  31.2 us (95%)
  local copies, waits for them, and re-layouts  0.65 us (2%)
  between operations  0.65 us (2%)
    pallas_call x1, Pallas kernels, shards(): pl.pallas_call(functools.partial(fused_kernel, slots, positions, features...  30.4 us
    pallas_call x1, Pallas kernels, shards(): pl.pallas_call(leave_kernel, out_shape=(grad_shape, total_shape), in_spec...  0.81 us

profile of v4, /device:TPU:0, one launch (start us, length us, event | category | flops | bytes accessed | tf_op | source)
XLA Modules:
  0.0 32.5 jit_solution(17918712244563484174)
XLA Ops:
  0.6 0.0 copy-start
  0.6 0.6 %copy-done = s32[1,1,6]{2,1,0:T(1,128)S(1)} copy-done((s32[1,1,6]{2,1,0:T(1,128)S(1)}, s32[1,1,6]{2,1,0:T(1,128)}, u32[]{:S(2)}) %copy-start) | copy-done | bytes 48
  1.3 30.4 %fused.1 = (bf16[1,1,6,64,512]{4,3,2,1,0:T(8,128)(2,1)S(1)}, f32[128,256]{1,0:T(8,128)S(1)}) custom-call(s32[1,1,6]{2,1,0:T(1,128)S(1)} %copy-done, bf16[1,1,6,64,512]{4,3,2,1,0:T(8,128)(2,1)} %hist_hbm.1, bf16[1,1,6,64,512]{4,3,2,1,0:T(8,128)(2,1)} %cot_hbm.1, bf16[512,2048]{1,0:T(8,128)(2,1)} %win_hbm.1, bf16[512,512]{1,0:T(8,128)(2,1)} %wout_hbm.1), custom_call_target="tpu_custom_call" | custom-call | tf_op jit(solution)/shard_map/fused/pallas_call | solution.py:350
  31.7 0.8 %leave.1 = (bf16[1,1,6,64,512]{4,3,2,1,0:T(8,128)(2,1)}, f32[128,256]{1,0:T(8,128)}) custom-call(bf16[1,1,6,64,512]{4,3,2,1,0:T(8,128)(2,1)S(1)} %get-tuple-element.4.grad_in, f32[128,256]{1,0:T(8,128)S(1)} %get-tuple-element.5.total_in), custom_call_target="tpu_custom_call" | custom-call | tf_op jit(solution)/shard_map/leave/pallas_call | solution.py:361
Async XLA Ops:
  0.6 0.7 %copy-start = (s32[1,1,6]{2,1,0:T(1,128)S(1)}, s32[1,1,6]{2,1,0:T(1,128)}, u32[]{:S(2)}) copy-start(s32[1,1,6]{2,1,0:T(1,128)} %lens_ref.1) | copy-start | bytes 76
